TPU v7x, 32 devices: a whole 2x2x4 slice. The times are simulated.
32 devices in a mesh: depth: 8 (over z, y), lat: 4 (over x, core).
Axes of the slice: x: 2, y: 2, z: 4, core: 2. Of those that a mesh axis runs over, the one named last changes fastest.
Arguments:
- right_sides: bfloat16 [16, 2, 64, 3072], P('depth', None, None, 'lat'), may hold values from -6 to 6
- sources: int32 [64], replicated, may hold values from 0 to 3071
- coupling: float32 [16, 3072], P('depth', 'lat'), may hold values from 0.76 to 0.86
- block_cols: int32 [16, 24, 4], P('depth', 'lat'), may hold values from 0 to 23, as said below
- factors: bfloat16 [16, 24, 4, 2, 128, 128], P('depth', 'lat'), may hold values from -0.2 to 1.2
Outputs:
- solution: bfloat16 [16, 2, 64, 3072], P('depth', None, None, 'lat')
Inputs may be any that keep to these rules, and one draw needn't show every extreme that they name: block_cols[k, r, 0] is r; the entries of a row are distinct and within 3 of r.
All inputs are finite; a program needn't handle non-finite values.
Results may differ from a plain program's by a relative error of at most 0.03.
Values may be sent and summed in bfloat16 or wider, within the bound.
A program may use at most 64 MiB of HBM per device.

v0:
```python
import jax
import jax.numpy as jnp
from jax import lax
from jax.sharding import PartitionSpec as P

REACH = 3
FRONT = 16


source_gain = 8.0


def extended_2(block, sides, width):
    for axis, dim in sides:
        count = lax.axis_size(axis)
        forward = [(i, i + 1) for i in range(count - 1)]
        backward = [(target, source) for source, target in forward]
        low = lax.ppermute(
            lax.slice_in_dim(block, block.shape[dim] - width, None, axis=dim), axis, forward
        )
        high = lax.ppermute(lax.slice_in_dim(block, 0, width, axis=dim), axis, backward)
        block = jnp.concatenate([low, block, high], axis=dim)
    return block


def from_behind(block, axis, distance):
    devices = range(lax.axis_size(axis))
    route = [(i - distance, i) for i in devices if i - distance in devices]
    return lax.ppermute(block, axis, route)


def per_device(right_sides, sources, coupling, block_cols, factors):
    layers_dev = right_sides.shape[0]
    shot_count = right_sides.shape[2]
    tile_cells = right_sides.shape[3]
    block_rows = block_cols.shape[1]
    block_size = factors.shape[-1]
    stored_count = block_cols.shape[2]
    halo_cells = REACH * block_size
    depth_count = lax.axis_size("depth")
    depth_pos = lax.axis_index("depth")
    lat_pos = lax.axis_index("lat")
    offsets = (block_cols - (lat_pos * block_rows - REACH)).reshape(
        layers_dev, block_rows * stored_count
    )
    cell_ids = lat_pos * tile_cells + lax.iota(jnp.int32, tile_cells)
    spikes = jnp.where(cell_ids[None, :] == sources[:, None], source_gain, 0.0).astype(jnp.float32)
    front_size = FRONT
    front_count = shot_count // front_size
    turn_count = depth_count + front_count - 1

    def apply_factor(extended, layer_idx):
        pieces = extended.reshape(2, front_size, -1, block_size)
        picked = jnp.take(pieces, offsets[layer_idx], axis=2).reshape(
            2, front_size, block_rows, stored_count, block_size
        )
        product = jnp.einsum(
            "psrnj,rnqji->pqsri", picked, factors[layer_idx], preferred_element_type=jnp.float32
        )
        real_part = product[0, 0] - product[1, 1]
        imag_part = product[0, 1] + product[1, 0]
        return jnp.stack([real_part, imag_part]).reshape(2, front_size, tile_cells)

    def guarded(active, extended, layer_idx):
        return lax.cond(
            active,
            lambda: apply_factor(extended, layer_idx),
            lambda: jnp.zeros((2, front_size, tile_cells), jnp.float32),
        )

    def place(stored, piece, active, layer_idx, front_start):
        current = lax.dynamic_slice(
            stored, (layer_idx, 0, front_start, 0), (1, 2, front_size, tile_cells)
        )
        chosen = jnp.where(active, piece[None], current)
        return lax.dynamic_update_slice(stored, chosen, (layer_idx, 0, front_start, 0))

    def down_turn(turn_idx, state_pair):
        inbound, stored = state_pair
        front_slot = turn_idx - depth_pos
        active = (front_slot >= 0) & (front_slot < front_count)
        front_start = jnp.clip(front_slot, 0, front_count - 1) * front_size
        front_spikes = lax.dynamic_slice_in_dim(spikes, front_start, front_size, 0)
        previous = inbound
        for layer_idx in range(layers_dev):
            source_load = lax.dynamic_slice_in_dim(
                right_sides[layer_idx], front_start, front_size, 1
            ).astype(jnp.float32)
            source_load = source_load.at[0].add(front_spikes)
            mixed_in = (
                source_load - coupling[layer_idx][None, None, :] * previous.astype(jnp.float32)
            ).astype(jnp.bfloat16)
            extended = extended_2(mixed_in, (("lat", 2),), halo_cells)
            previous = guarded(active, extended, layer_idx).astype(jnp.bfloat16)
            stored = place(stored, previous, active, layer_idx, front_start)
        outbound = from_behind(previous, "depth", 1)
        return (outbound, stored)

    empty_front = jnp.zeros((2, front_size, tile_cells), jnp.bfloat16)
    empty_all = jnp.zeros((layers_dev, 2, shot_count, tile_cells), jnp.bfloat16)
    _, stored = lax.fori_loop(0, turn_count, down_turn, (empty_front, empty_all))

    def up_turn(turn_idx, state_pair):
        inbound, result = state_pair
        front_slot = turn_idx - (depth_count - 1 - depth_pos)
        active = (front_slot >= 0) & (front_slot < front_count)
        front_start = jnp.clip(front_slot, 0, front_count - 1) * front_size
        handed = inbound
        for layer_idx in reversed(range(layers_dev)):
            extended = extended_2(handed, (("lat", 2),), halo_cells)
            correction = guarded(active, extended, layer_idx)
            down_part = lax.dynamic_slice_in_dim(
                stored[layer_idx], front_start, front_size, 1
            ).astype(jnp.float32)
            updated = (down_part - correction).astype(jnp.bfloat16)
            result = place(result, updated, active, layer_idx, front_start)
            handed = (coupling[layer_idx][None, None, :] * updated.astype(jnp.float32)).astype(
                jnp.bfloat16
            )
        outbound = from_behind(handed, "depth", -1)
        return (outbound, result)

    _, solution = lax.fori_loop(0, turn_count, up_turn, (empty_front, empty_all))
    return solution


def solution(mesh):
    in_specs = (
        P("depth", None, None, "lat"),
        P(),
        P("depth", "lat"),
        P("depth", "lat", None),
        P("depth", "lat", None, None, None, None),
    )
    out_specs = P("depth", None, None, "lat")
    return jax.shard_map(
        per_device, mesh=mesh, in_specs=in_specs, out_specs=out_specs, check_vma=False
    )
```

profile of v0, /device:TPU:1, one launch (start us, length us, event | category | flops | bytes accessed | tf_op | source)
XLA Modules:
  0.0 607.0 jit_solution(14161686457472017742)
XLA Ops:
  6.6 303.6 %while.36 = (s32[]{:T(128)}, bf16[2,16,768]{2,1,0:T(8,128)(2,1)}, bf16[2,2,64,768]{3,2,1,0:T(8,128)(2,1)}, s32[]{:T(128)}, bf16[2,2,64,768]{3,2,1,0:T(8,128)(2,1...) while((s32[]{:T(128)}, bf16[2,16,768]{2,1,0:T(8,128)(2,1)}, ...), condition=%wide.region_5.7_spmd, body=%wide.region_0.6_spmd.sunk | while | flops 101968176 | bytes 11480507 | solution.py:101
  11.3 4.5 collective-permute-start.1
  66.9 4.2 collective-permute-start.1
  96.1 4.2 collective-permute-start.1
  125.2 4.2 collective-permute-start.1
  133.9 4.2 collective-permute-start.3
  139.6 7.9 %collective-permute-start.4 = (bf16[2,16,768]{2,1,0:T(8,128)(2,1)S(1)}, bf16[2,16,768]{2,1,0:T(8,128)(2,1)S(1)}, u32[]{:S(2)}, u32[]{:S(2)}) collective-permute-start(bf16[2,16,768]{2,1,0:T(8,128)(2,1)S(1)} %get-tuple-element.795), channel_id=1, source_target_pairs={{0,4},{4,8},{8,12},{12,16},{16,20},{20,24},{24,28},{1,5},{5,9},{9,... | collective-permute-start | bytes 147464 | tf_op jit(solution)/shard_map/while/body/eval_jaxpr/ppermute | solution.py:29
  154.4 4.2 collective-permute-start.1
  168.8 4.3 collective-permute-start.4
  179.9 4.3 collective-permute-start.1
  194.4 8.8 %collective-permute-start.4 = (bf16[2,16,768]{2,1,0:T(8,128)(2,1)S(1)}, bf16[2,16,768]{2,1,0:T(8,128)(2,1)S(1)}, u32[]{:S(2)}, u32[]{:S(2)}) collective-permute-start(bf16[2,16,768]{2,1,0:T(8,128)(2,1)S(1)} %get-tuple-element.795), channel_id=1, source_target_pairs={{0,4},{4,8},{8,12},{12,16},{16,20},{20,24},{24,28},{1,5},{5,9},{9,... | collective-permute-start | bytes 147464 | tf_op jit(solution)/shard_map/while/body/eval_jaxpr/ppermute | solution.py:29
  210.0 4.3 collective-permute-start.1
  224.4 4.9 collective-permute-start.4
  236.1 4.3 collective-permute-start.1
  250.5 4.9 collective-permute-start.4
  262.2 4.3 collective-permute-start.1
  276.7 4.9 collective-permute-start.4
  288.4 4.3 collective-permute-start.1
  302.8 5.3 collective-permute-start.4
  311.0 296.0 %while.37 = (s32[]{:T(128)}, bf16[2,16,768]{2,1,0:T(8,128)(2,1)S(1)}, bf16[2,2,64,768]{3,2,1,0:T(8,128)(2,1)}, f32[2,768]{1,0:T(2,128)S(1)}, bf16[2,2,64,768]{3,...) while((s32[]{:T(128)}, ...), condition=%wide.region_11.13_spmd, body=%wide.region_6.12_spmd.sunk | while | flops 102041896 | bytes 10546539 | solution.py:123
  312.9 4.3 collective-permute-start.6
  336.2 4.5 collective-permute-start.6
  359.7 4.5 collective-permute-start.6
  383.2 4.5 collective-permute-start.6
  407.2 4.5 collective-permute-start.6
  430.7 4.5 collective-permute-start.6
  454.2 4.5 collective-permute-start.6
  472.2 28.1 %collective-permute-done.9 = bf16[2,16,768]{2,1,0:T(8,128)(2,1)S(1)} collective-permute-done((bf16[2,16,768]{2,1,0:T(8,128)(2,1)S(1)}, bf16[2,16,768]{2,1,0:T(8,128)(2,1)S(1)}, u32[]{:S(2)}, u32[]{:S(2)}) %collective-permute-start.9) | collective-permute-done | bytes 49184 | tf_op jit(solution)/shard_map/while/body/eval_jaxpr/ppermute | solution.py:29
  502.3 4.5 collective-permute-start.6
  529.2 4.5 collective-permute-start.6
  556.2 4.5 collective-permute-start.6
  583.1 4.5 collective-permute-start.6
  (782 shorter events, 475.2 us)
Async XLA Ops:
  20.3 7.6 %collective-permute-start.2 = (bf16[2,16,384]{2,1,0:T(8,128)(2,1)S(1)}, bf16[2,16,384]{2,1,0:T(8,128)(2,1)S(1)}, u32[]{:S(2)}, u32[]{:S(2)}) collective-permute-start(bf16[2,16,384]{2,1,0:T(8,128)(2,1)S(1)} %get-tuple-element.793), channel_id=1, source_target_pairs={{1,0},{2,1},{3,2},{5,4},{6,5},{7,6},{9,8},{10,9},{11,10},{13,12},{... | collective-permute-start | bytes 73736 | tf_op jit(solution)/shard_map/while/body/eval_jaxpr/ppermute | solution.py:21
  46.5 7.6 %collective-permute-start.2 = (bf16[2,16,384]{2,1,0:T(8,128)(2,1)S(1)}, bf16[2,16,384]{2,1,0:T(8,128)(2,1)S(1)}, u32[]{:S(2)}, u32[]{:S(2)}) collective-permute-start(bf16[2,16,384]{2,1,0:T(8,128)(2,1)S(1)} %get-tuple-element.793), channel_id=1, source_target_pairs={{1,0},{2,1},{3,2},{5,4},{6,5},{7,6},{9,8},{10,9},{11,10},{13,12},{... | collective-permute-start | bytes 73736 | tf_op jit(solution)/shard_map/while/body/eval_jaxpr/ppermute | solution.py:21
  75.6 7.6 %collective-permute-start.2 = (bf16[2,16,384]{2,1,0:T(8,128)(2,1)S(1)}, bf16[2,16,384]{2,1,0:T(8,128)(2,1)S(1)}, u32[]{:S(2)}, u32[]{:S(2)}) collective-permute-start(bf16[2,16,384]{2,1,0:T(8,128)(2,1)S(1)} %get-tuple-element.793), channel_id=1, source_target_pairs={{1,0},{2,1},{3,2},{5,4},{6,5},{7,6},{9,8},{10,9},{11,10},{13,12},{... | collective-permute-start | bytes 73736 | tf_op jit(solution)/shard_map/while/body/eval_jaxpr/ppermute | solution.py:21
  104.8 7.6 %collective-permute-start.2 = (bf16[2,16,384]{2,1,0:T(8,128)(2,1)S(1)}, bf16[2,16,384]{2,1,0:T(8,128)(2,1)S(1)}, u32[]{:S(2)}, u32[]{:S(2)}) collective-permute-start(bf16[2,16,384]{2,1,0:T(8,128)(2,1)S(1)} %get-tuple-element.793), channel_id=1, source_target_pairs={{1,0},{2,1},{3,2},{5,4},{6,5},{7,6},{9,8},{10,9},{11,10},{13,12},{... | collective-permute-start | bytes 73736 | tf_op jit(solution)/shard_map/while/body/eval_jaxpr/ppermute | solution.py:21
  132.0 7.6 %collective-permute-start.2 = (bf16[2,16,384]{2,1,0:T(8,128)(2,1)S(1)}, bf16[2,16,384]{2,1,0:T(8,128)(2,1)S(1)}, u32[]{:S(2)}, u32[]{:S(2)}) collective-permute-start(bf16[2,16,384]{2,1,0:T(8,128)(2,1)S(1)} %get-tuple-element.793), channel_id=1, source_target_pairs={{1,0},{2,1},{3,2},{5,4},{6,5},{7,6},{9,8},{10,9},{11,10},{13,12},{... | collective-permute-start | bytes 73736 | tf_op jit(solution)/shard_map/while/body/eval_jaxpr/ppermute | solution.py:21
  139.6 9.4 %collective-permute-start.4 = (bf16[2,16,768]{2,1,0:T(8,128)(2,1)S(1)}, bf16[2,16,768]{2,1,0:T(8,128)(2,1)S(1)}, u32[]{:S(2)}, u32[]{:S(2)}) collective-permute-start(bf16[2,16,768]{2,1,0:T(8,128)(2,1)S(1)} %get-tuple-element.795), channel_id=1, source_target_pairs={{0,4},{4,8},{8,12},{12,16},{16,20},{20,24},{24,28},{1,5},{5,9},{9,... | collective-permute-start | bytes 147464 | tf_op jit(solution)/shard_map/while/body/eval_jaxpr/ppermute | solution.py:29
  161.1 7.6 %collective-permute-start.2 = (bf16[2,16,384]{2,1,0:T(8,128)(2,1)S(1)}, bf16[2,16,384]{2,1,0:T(8,128)(2,1)S(1)}, u32[]{:S(2)}, u32[]{:S(2)}) collective-permute-start(bf16[2,16,384]{2,1,0:T(8,128)(2,1)S(1)} %get-tuple-element.793), channel_id=1, source_target_pairs={{1,0},{2,1},{3,2},{5,4},{6,5},{7,6},{9,8},{10,9},{11,10},{13,12},{... | collective-permute-start | bytes 73736 | tf_op jit(solution)/shard_map/while/body/eval_jaxpr/ppermute | solution.py:21
  186.7 7.6 %collective-permute-start.2 = (bf16[2,16,384]{2,1,0:T(8,128)(2,1)S(1)}, bf16[2,16,384]{2,1,0:T(8,128)(2,1)S(1)}, u32[]{:S(2)}, u32[]{:S(2)}) collective-permute-start(bf16[2,16,384]{2,1,0:T(8,128)(2,1)S(1)} %get-tuple-element.793), channel_id=1, source_target_pairs={{1,0},{2,1},{3,2},{5,4},{6,5},{7,6},{9,8},{10,9},{11,10},{13,12},{... | collective-permute-start | bytes 73736 | tf_op jit(solution)/shard_map/while/body/eval_jaxpr/ppermute | solution.py:21
  194.4 10.2 %collective-permute-start.4 = (bf16[2,16,768]{2,1,0:T(8,128)(2,1)S(1)}, bf16[2,16,768]{2,1,0:T(8,128)(2,1)S(1)}, u32[]{:S(2)}, u32[]{:S(2)}) collective-permute-start(bf16[2,16,768]{2,1,0:T(8,128)(2,1)S(1)} %get-tuple-element.795), channel_id=1, source_target_pairs={{0,4},{4,8},{8,12},{12,16},{16,20},{20,24},{24,28},{1,5},{5,9},{9,... | collective-permute-start | bytes 147464 | tf_op jit(solution)/shard_map/while/body/eval_jaxpr/ppermute | solution.py:29
  216.8 7.6 %collective-permute-start.2 = (bf16[2,16,384]{2,1,0:T(8,128)(2,1)S(1)}, bf16[2,16,384]{2,1,0:T(8,128)(2,1)S(1)}, u32[]{:S(2)}, u32[]{:S(2)}) collective-permute-start(bf16[2,16,384]{2,1,0:T(8,128)(2,1)S(1)} %get-tuple-element.793), channel_id=1, source_target_pairs={{1,0},{2,1},{3,2},{5,4},{6,5},{7,6},{9,8},{10,9},{11,10},{13,12},{... | collective-permute-start | bytes 73736 | tf_op jit(solution)/shard_map/while/body/eval_jaxpr/ppermute | solution.py:21
  242.9 7.6 %collective-permute-start.2 = (bf16[2,16,384]{2,1,0:T(8,128)(2,1)S(1)}, bf16[2,16,384]{2,1,0:T(8,128)(2,1)S(1)}, u32[]{:S(2)}, u32[]{:S(2)}) collective-permute-start(bf16[2,16,384]{2,1,0:T(8,128)(2,1)S(1)} %get-tuple-element.793), channel_id=1, source_target_pairs={{1,0},{2,1},{3,2},{5,4},{6,5},{7,6},{9,8},{10,9},{11,10},{13,12},{... | collective-permute-start | bytes 73736 | tf_op jit(solution)/shard_map/while/body/eval_jaxpr/ppermute | solution.py:21
  269.0 7.6 %collective-permute-start.2 = (bf16[2,16,384]{2,1,0:T(8,128)(2,1)S(1)}, bf16[2,16,384]{2,1,0:T(8,128)(2,1)S(1)}, u32[]{:S(2)}, u32[]{:S(2)}) collective-permute-start(bf16[2,16,384]{2,1,0:T(8,128)(2,1)S(1)} %get-tuple-element.793), channel_id=1, source_target_pairs={{1,0},{2,1},{3,2},{5,4},{6,5},{7,6},{9,8},{10,9},{11,10},{13,12},{... | collective-permute-start | bytes 73736 | tf_op jit(solution)/shard_map/while/body/eval_jaxpr/ppermute | solution.py:21
  295.1 7.6 %collective-permute-start.2 = (bf16[2,16,384]{2,1,0:T(8,128)(2,1)S(1)}, bf16[2,16,384]{2,1,0:T(8,128)(2,1)S(1)}, u32[]{:S(2)}, u32[]{:S(2)}) collective-permute-start(bf16[2,16,384]{2,1,0:T(8,128)(2,1)S(1)} %get-tuple-element.793), channel_id=1, source_target_pairs={{1,0},{2,1},{3,2},{5,4},{6,5},{7,6},{9,8},{10,9},{11,10},{13,12},{... | collective-permute-start | bytes 73736 | tf_op jit(solution)/shard_map/while/body/eval_jaxpr/ppermute | solution.py:21
  311.0 8.1 %collective-permute-start.5 = (bf16[2,16,384]{2,1,0:T(8,128)(2,1)S(1)}, bf16[2,16,384]{2,1,0:T(8,128)(2,1)S(1)}, u32[]{:S(2)}, u32[]{:S(2)}) collective-permute-start(bf16[2,16,384]{2,1,0:T(8,128)(2,1)S(1)} %get-tuple-element.808), channel_id=1, source_target_pairs={{1,0},{2,1},{3,2},{5,4},{6,5},{7,6},{9,8},{10,9},{11,10},{13,12},{... | collective-permute-start | bytes 73736 | tf_op jit(solution)/shard_map/while/body/eval_jaxpr/ppermute | solution.py:21
  320.0 7.1 %collective-permute-start.7 = (bf16[2,16,384]{2,1,0:T(8,128)(2,1)S(1)}, bf16[2,16,384]{2,1,0:T(8,128)(2,1)S(1)}, u32[]{:S(2)}, u32[]{:S(2)}) collective-permute-start(bf16[2,16,384]{2,1,0:T(8,128)(2,1)S(1)} %get-tuple-element.811), channel_id=1, source_target_pairs={{1,0},{2,1},{3,2},{5,4},{6,5},{7,6},{9,8},{10,9},{11,10},{13,12},{... | collective-permute-start | bytes 73736 | tf_op jit(solution)/shard_map/while/body/eval_jaxpr/ppermute | solution.py:21
  334.2 8.3 %collective-permute-start.5 = (bf16[2,16,384]{2,1,0:T(8,128)(2,1)S(1)}, bf16[2,16,384]{2,1,0:T(8,128)(2,1)S(1)}, u32[]{:S(2)}, u32[]{:S(2)}) collective-permute-start(bf16[2,16,384]{2,1,0:T(8,128)(2,1)S(1)} %get-tuple-element.808), channel_id=1, source_target_pairs={{1,0},{2,1},{3,2},{5,4},{6,5},{7,6},{9,8},{10,9},{11,10},{13,12},{... | collective-permute-start | bytes 73736 | tf_op jit(solution)/shard_map/while/body/eval_jaxpr/ppermute | solution.py:21
  343.5 7.1 %collective-permute-start.7 = (bf16[2,16,384]{2,1,0:T(8,128)(2,1)S(1)}, bf16[2,16,384]{2,1,0:T(8,128)(2,1)S(1)}, u32[]{:S(2)}, u32[]{:S(2)}) collective-permute-start(bf16[2,16,384]{2,1,0:T(8,128)(2,1)S(1)} %get-tuple-element.811), channel_id=1, source_target_pairs={{1,0},{2,1},{3,2},{5,4},{6,5},{7,6},{9,8},{10,9},{11,10},{13,12},{... | collective-permute-start | bytes 73736 | tf_op jit(solution)/shard_map/while/body/eval_jaxpr/ppermute | solution.py:21
  357.8 8.3 %collective-permute-start.5 = (bf16[2,16,384]{2,1,0:T(8,128)(2,1)S(1)}, bf16[2,16,384]{2,1,0:T(8,128)(2,1)S(1)}, u32[]{:S(2)}, u32[]{:S(2)}) collective-permute-start(bf16[2,16,384]{2,1,0:T(8,128)(2,1)S(1)} %get-tuple-element.808), channel_id=1, source_target_pairs={{1,0},{2,1},{3,2},{5,4},{6,5},{7,6},{9,8},{10,9},{11,10},{13,12},{... | collective-permute-start | bytes 73736 | tf_op jit(solution)/shard_map/while/body/eval_jaxpr/ppermute | solution.py:21
  367.0 7.1 %collective-permute-start.7 = (bf16[2,16,384]{2,1,0:T(8,128)(2,1)S(1)}, bf16[2,16,384]{2,1,0:T(8,128)(2,1)S(1)}, u32[]{:S(2)}, u32[]{:S(2)}) collective-permute-start(bf16[2,16,384]{2,1,0:T(8,128)(2,1)S(1)} %get-tuple-element.811), channel_id=1, source_target_pairs={{1,0},{2,1},{3,2},{5,4},{6,5},{7,6},{9,8},{10,9},{11,10},{13,12},{... | collective-permute-start | bytes 73736 | tf_op jit(solution)/shard_map/while/body/eval_jaxpr/ppermute | solution.py:21
  381.3 8.3 %collective-permute-start.5 = (bf16[2,16,384]{2,1,0:T(8,128)(2,1)S(1)}, bf16[2,16,384]{2,1,0:T(8,128)(2,1)S(1)}, u32[]{:S(2)}, u32[]{:S(2)}) collective-permute-start(bf16[2,16,384]{2,1,0:T(8,128)(2,1)S(1)} %get-tuple-element.808), channel_id=1, source_target_pairs={{1,0},{2,1},{3,2},{5,4},{6,5},{7,6},{9,8},{10,9},{11,10},{13,12},{... | collective-permute-start | bytes 73736 | tf_op jit(solution)/shard_map/while/body/eval_jaxpr/ppermute | solution.py:21
  390.5 7.1 %collective-permute-start.7 = (bf16[2,16,384]{2,1,0:T(8,128)(2,1)S(1)}, bf16[2,16,384]{2,1,0:T(8,128)(2,1)S(1)}, u32[]{:S(2)}, u32[]{:S(2)}) collective-permute-start(bf16[2,16,384]{2,1,0:T(8,128)(2,1)S(1)} %get-tuple-element.811), channel_id=1, source_target_pairs={{1,0},{2,1},{3,2},{5,4},{6,5},{7,6},{9,8},{10,9},{11,10},{13,12},{... | collective-permute-start | bytes 73736 | tf_op jit(solution)/shard_map/while/body/eval_jaxpr/ppermute | solution.py:21
  405.3 8.3 %collective-permute-start.5 = (bf16[2,16,384]{2,1,0:T(8,128)(2,1)S(1)}, bf16[2,16,384]{2,1,0:T(8,128)(2,1)S(1)}, u32[]{:S(2)}, u32[]{:S(2)}) collective-permute-start(bf16[2,16,384]{2,1,0:T(8,128)(2,1)S(1)} %get-tuple-element.808), channel_id=1, source_target_pairs={{1,0},{2,1},{3,2},{5,4},{6,5},{7,6},{9,8},{10,9},{11,10},{13,12},{... | collective-permute-start | bytes 73736 | tf_op jit(solution)/shard_map/while/body/eval_jaxpr/ppermute | solution.py:21
  428.8 8.3 %collective-permute-start.5 = (bf16[2,16,384]{2,1,0:T(8,128)(2,1)S(1)}, bf16[2,16,384]{2,1,0:T(8,128)(2,1)S(1)}, u32[]{:S(2)}, u32[]{:S(2)}) collective-permute-start(bf16[2,16,384]{2,1,0:T(8,128)(2,1)S(1)} %get-tuple-element.808), channel_id=1, source_target_pairs={{1,0},{2,1},{3,2},{5,4},{6,5},{7,6},{9,8},{10,9},{11,10},{13,12},{... | collective-permute-start | bytes 73736 | tf_op jit(solution)/shard_map/while/body/eval_jaxpr/ppermute | solution.py:21
  438.0 7.1 %collective-permute-start.7 = (bf16[2,16,384]{2,1,0:T(8,128)(2,1)S(1)}, bf16[2,16,384]{2,1,0:T(8,128)(2,1)S(1)}, u32[]{:S(2)}, u32[]{:S(2)}) collective-permute-start(bf16[2,16,384]{2,1,0:T(8,128)(2,1)S(1)} %get-tuple-element.811), channel_id=1, source_target_pairs={{1,0},{2,1},{3,2},{5,4},{6,5},{7,6},{9,8},{10,9},{11,10},{13,12},{... | collective-permute-start | bytes 73736 | tf_op jit(solution)/shard_map/while/body/eval_jaxpr/ppermute | solution.py:21
  452.3 8.3 %collective-permute-start.5 = (bf16[2,16,384]{2,1,0:T(8,128)(2,1)S(1)}, bf16[2,16,384]{2,1,0:T(8,128)(2,1)S(1)}, u32[]{:S(2)}, u32[]{:S(2)}) collective-permute-start(bf16[2,16,384]{2,1,0:T(8,128)(2,1)S(1)} %get-tuple-element.808), channel_id=1, source_target_pairs={{1,0},{2,1},{3,2},{5,4},{6,5},{7,6},{9,8},{10,9},{11,10},{13,12},{... | collective-permute-start | bytes 73736 | tf_op jit(solution)/shard_map/while/body/eval_jaxpr/ppermute | solution.py:21
  469.5 30.9 %collective-permute-start.9 = (bf16[2,16,768]{2,1,0:T(8,128)(2,1)S(1)}, bf16[2,16,768]{2,1,0:T(8,128)(2,1)S(1)}, u32[]{:S(2)}, u32[]{:S(2)}) collective-permute-start(bf16[2,16,768]{2,1,0:T(8,128)(2,1)S(1)} %multiply_convert_fusion.5), channel_id=1, source_target_pairs={{4,0},{8,4},{12,8},{16,12},{20,16},{24,20},{28,24},{5,1},{9,5},{13... | collective-permute-start | bytes 147464 | tf_op jit(solution)/shard_map/while/body/eval_jaxpr/ppermute | solution.py:29
  500.4 8.3 %collective-permute-start.5 = (bf16[2,16,384]{2,1,0:T(8,128)(2,1)S(1)}, bf16[2,16,384]{2,1,0:T(8,128)(2,1)S(1)}, u32[]{:S(2)}, u32[]{:S(2)}) collective-permute-start(bf16[2,16,384]{2,1,0:T(8,128)(2,1)S(1)} %get-tuple-element.808), channel_id=1, source_target_pairs={{1,0},{2,1},{3,2},{5,4},{6,5},{7,6},{9,8},{10,9},{11,10},{13,12},{... | collective-permute-start | bytes 73736 | tf_op jit(solution)/shard_map/while/body/eval_jaxpr/ppermute | solution.py:21
  527.3 8.3 %collective-permute-start.5 = (bf16[2,16,384]{2,1,0:T(8,128)(2,1)S(1)}, bf16[2,16,384]{2,1,0:T(8,128)(2,1)S(1)}, u32[]{:S(2)}, u32[]{:S(2)}) collective-permute-start(bf16[2,16,384]{2,1,0:T(8,128)(2,1)S(1)} %get-tuple-element.808), channel_id=1, source_target_pairs={{1,0},{2,1},{3,2},{5,4},{6,5},{7,6},{9,8},{10,9},{11,10},{13,12},{... | collective-permute-start | bytes 73736 | tf_op jit(solution)/shard_map/while/body/eval_jaxpr/ppermute | solution.py:21
  538.4 7.1 %collective-permute-start.7 = (bf16[2,16,384]{2,1,0:T(8,128)(2,1)S(1)}, bf16[2,16,384]{2,1,0:T(8,128)(2,1)S(1)}, u32[]{:S(2)}, u32[]{:S(2)}) collective-permute-start(bf16[2,16,384]{2,1,0:T(8,128)(2,1)S(1)} %get-tuple-element.811), channel_id=1, source_target_pairs={{1,0},{2,1},{3,2},{5,4},{6,5},{7,6},{9,8},{10,9},{11,10},{13,12},{... | collective-permute-start | bytes 73736 | tf_op jit(solution)/shard_map/while/body/eval_jaxpr/ppermute | solution.py:21
  554.3 8.3 %collective-permute-start.5 = (bf16[2,16,384]{2,1,0:T(8,128)(2,1)S(1)}, bf16[2,16,384]{2,1,0:T(8,128)(2,1)S(1)}, u32[]{:S(2)}, u32[]{:S(2)}) collective-permute-start(bf16[2,16,384]{2,1,0:T(8,128)(2,1)S(1)} %get-tuple-element.808), channel_id=1, source_target_pairs={{1,0},{2,1},{3,2},{5,4},{6,5},{7,6},{9,8},{10,9},{11,10},{13,12},{... | collective-permute-start | bytes 73736 | tf_op jit(solution)/shard_map/while/body/eval_jaxpr/ppermute | solution.py:21
  565.4 7.1 %collective-permute-start.7 = (bf16[2,16,384]{2,1,0:T(8,128)(2,1)S(1)}, bf16[2,16,384]{2,1,0:T(8,128)(2,1)S(1)}, u32[]{:S(2)}, u32[]{:S(2)}) collective-permute-start(bf16[2,16,384]{2,1,0:T(8,128)(2,1)S(1)} %get-tuple-element.811), channel_id=1, source_target_pairs={{1,0},{2,1},{3,2},{5,4},{6,5},{7,6},{9,8},{10,9},{11,10},{13,12},{... | collective-permute-start | bytes 73736 | tf_op jit(solution)/shard_map/while/body/eval_jaxpr/ppermute | solution.py:21
  581.2 8.3 %collective-permute-start.5 = (bf16[2,16,384]{2,1,0:T(8,128)(2,1)S(1)}, bf16[2,16,384]{2,1,0:T(8,128)(2,1)S(1)}, u32[]{:S(2)}, u32[]{:S(2)}) collective-permute-start(bf16[2,16,384]{2,1,0:T(8,128)(2,1)S(1)} %get-tuple-element.808), channel_id=1, source_target_pairs={{1,0},{2,1},{3,2},{5,4},{6,5},{7,6},{9,8},{10,9},{11,10},{13,12},{... | collective-permute-start | bytes 73736 | tf_op jit(solution)/shard_map/while/body/eval_jaxpr/ppermute | solution.py:21
  (101 other events, 474.2 us)
where the time goes:
time: 617 us; the launch traced here: 607 us
  starting transfers between devices  335 us (54%)
  other arithmetic  128 us (21%)
  waiting for transfers between devices  72 us (12%)
  local copies, waits for them, and re-layouts  60.2 us (10%)
    ppermute x44, starting transfers between devices, extended_2(): lax.ppermute(lax.slice_in_dim(block, block.shape[dim] - width, None, axis...  183 us
    ppermute x44, starting transfers between devices, extended_2(): lax.ppermute(lax.slice_in_dim(block, 0, width, axis=dim), axis, backward)  84.4 us
    ppermute x22, starting transfers between devices, from_behind(): return lax.ppermute(block, axis, route)  68.4 us
    dynamic_update_slice x44, other arithmetic, place(): lax.dynamic_update_slice(stored, chosen, (layer_idx, 0, front_start, 0))  64.1 us
    ppermute x22, waiting for transfers between devices, from_behind(): return lax.ppermute(block, axis, route)  61.8 us
    slice x11, local copies, waits for them, and re-layouts, up_turn(): stored[layer_idx]  19.9 us
    convert_element_type x22, other arithmetic, down_turn(): mixed_in = (source_load - coupling[layer_idx][None, None, :] * previous.a...  19.4 us
    convert_element_type x22, other arithmetic, up_turn(): (coupling[layer_idx][None, None, :] * updated.astype(jnp.float32)).astype...  18.2 us
  transfers between devices with their start and end apart: 110, of which 22 were waited for; matrix products, arithmetic and copies ran while one was open for 14% of the time, Pallas kernels for 0%

commit v1 on v0

v1 whole, which is shorter than its diff:
```python
import functools

import jax
import jax.numpy as jnp
from jax import lax
from jax.experimental import pallas as pl
from jax.experimental.pallas import tpu as pltpu
from jax.sharding import PartitionSpec as P

REACH = 3
FRONTS = 4

source_gain = 8.0

MESH = pl.DeviceIdType.MESH


def sweep_kernel(
    depth_count, lat_count, fronts,
    cols_ref, srcs_ref, rhs_ref, coup_ref, fac_ref, out_ref,
    ext, din, uin, dmid, umid, wa, wb, mixed, handed, hout, rhalo, chalo,
    d_send, d_recv, u_send, u_recv, dm_send, dm_recv, um_send, um_recv, p_send, p_recv,
):
    d = lax.axis_index("depth")
    l = lax.axis_index("lat")
    rows, stored, _, blk, _ = fac_ref.shape[1:]
    shots = rhs_ref.shape[2] // fronts
    ext_rows = rows + 2 * REACH
    halo = REACH * blk

    def valid(dd, dl):
        ok = jnp.bool_(True)
        if dd < 0:
            ok = d > 0
        if dd > 0:
            ok = d < depth_count - 1
        if dl < 0:
            ok = ok & (l > 0)
        if dl > 0:
            ok = ok & (l < lat_count - 1)
        return ok

    around = [(dd, dl) for dd in (-1, 0, 1) for dl in (-1, 0, 1) if (dd, dl) != (0, 0)]
    barrier = pltpu.get_barrier_semaphore()
    total = jnp.int32(0)
    for dd, dl in around:
        ok = valid(dd, dl)

        @pl.when(ok)
        def _():
            pl.semaphore_signal(barrier, inc=1, device_id=(d + dd, l + dl), device_id_type=MESH)

        total = total + ok.astype(jnp.int32)
    pl.semaphore_wait(barrier, total)

    def remote(src, dst, ssem, rsem, dd, dl):
        return pltpu.make_async_remote_copy(
            src_ref=src, dst_ref=dst, send_sem=ssem, recv_sem=rsem,
            device_id=(d + dd, l + dl), device_id_type=MESH,
        )

    def pre_copy(side, which):
        dl = 1 if side == 0 else -1
        lanes = pl.ds(rows * blk - halo, halo) if side == 0 else pl.ds(0, halo)
        if which == 0:
            src, dst = rhs_ref.at[0, :, :, lanes], rhalo.at[side]
        else:
            src, dst = coup_ref.at[:, lanes], chalo.at[side]
        i = 2 * side + which
        return remote(src, dst, p_send.at[i], p_recv.at[i], 0, dl)

    def mid_copy(f, side, src, dst, ssem, rsem):
        dl = 1 if side == 0 else -1
        first = rows - REACH if side == 0 else 0
        return remote(
            src.at[f, pl.ds(first, REACH)], dst.at[f, side], ssem.at[f, side], rsem.at[f, side], 0, dl
        )

    def depth_copy(f, slot, src, dst, ssem, rsem, dd):
        dl = 1 - slot
        if slot == 0:
            a, b, n = rows - REACH, 0, REACH
        elif slot == 1:
            a, b, n = 0, REACH, rows
        else:
            a, b, n = 0, REACH + rows, REACH
        return remote(
            src.at[f, pl.ds(a, n)], dst.at[f, pl.ds(b, n)], ssem.at[f, slot], rsem.at[f, slot], dd, dl
        )

    def to_dl(side):
        return 1 if side == 0 else -1

    for side in (0, 1):
        @pl.when(valid(0, to_dl(side)))
        def _():
            for which in (0, 1):
                pre_copy(side, which).start()

    lane = lax.broadcasted_iota(jnp.int32, (shots, blk), 1)
    first_cell = (l * rows - REACH) * blk

    def load_of(front, rhs, e):
        srcs = srcs_ref[front, :]
        spike = jnp.where(srcs == first_cell + e * blk + lane, source_gain, 0.0).astype(jnp.float32)
        value = rhs.astype(jnp.float32)
        return jnp.concatenate([value[0] + spike, value[1]], axis=0)

    def apply_row(layer, r):
        picks = [cols_ref[layer, r * stored + n] - l * rows + REACH for n in range(stored)]
        xs = [ext[jnp.clip(pick, 0, ext_rows - 1)] for pick in picks]
        x = jnp.concatenate(xs, axis=1)
        w = jnp.concatenate(
            [jnp.concatenate([fac_ref[layer, r, n, 0], fac_ref[layer, r, n, 1]], axis=1) for n in range(stored)],
            axis=0,
        )
        p = jnp.dot(x, w, preferred_element_type=jnp.float32)
        real = p[:shots, :blk] - p[shots:, blk:]
        imag = p[:shots, blk:] + p[shots:, :blk]
        return jnp.concatenate([real, imag], axis=0)

    def coup_of(layer, r):
        return coup_ref[pl.ds(layer, 1), pl.ds(r * blk, blk)]

    def depth_wait(f, dst, src, ssem, rsem, dd):
        for slot in (1, 0, 2):
            @pl.when(valid(dd, slot - 1))
            def _():
                depth_copy(f, slot, src, dst, ssem, rsem, -dd).wait_recv()

    def depth_start(f, dst, src, ssem, rsem, dd):
        for slot in (0, 2, 1):
            @pl.when(valid(dd, 1 - slot))
            def _():
                depth_copy(f, slot, src, dst, ssem, rsem, dd).start()

    def mid_start(f, src, dst, ssem, rsem):
        for side in (0, 1):
            @pl.when(valid(0, to_dl(side)))
            def _():
                mid_copy(f, side, src, dst, ssem, rsem).start()

    def mid_finish(f, src, dst, ssem, rsem):
        for r in range(rows):
            ext[REACH + r] = src[f, r]
        for side in (0, 1):
            @pl.when(valid(0, -to_dl(side)))
            def _():
                mid_copy(f, side, src, dst, ssem, rsem).wait_recv()
                for i in range(REACH):
                    e = i if side == 0 else REACH + rows + i
                    ext[e] = dst[f, side, i]

    def front_of(f):
        return pl.ds(pl.multiple_of(f * shots, shots), shots)

    def down_first(f):
        front = front_of(f)
        depth_wait(f, din, wb, d_send, d_recv, -1)

        def put(e, rhs, coup):
            previous = jnp.where(d > 0, din[f, e].astype(jnp.float32), 0.0)
            ext[e] = (load_of(front, rhs, e) - coup * previous).astype(jnp.bfloat16)

        for r in range(rows):
            put(REACH + r, rhs_ref[0, :, front, pl.ds(r * blk, blk)], coup_of(0, r))
        for side in (0, 1):
            @pl.when(valid(0, -to_dl(side)))
            def _():
                for i in range(REACH):
                    cells = pl.ds(i * blk, blk)
                    e = i if side == 0 else REACH + rows + i
                    put(e, rhalo[side, :, front, cells], chalo[side, pl.ds(0, 1), cells])
        for r in range(rows):
            w = apply_row(0, r).astype(jnp.bfloat16)
            wa[f, r] = w
            load = load_of(front, rhs_ref[1, :, front, pl.ds(r * blk, blk)], REACH + r)
            mixed[f, r] = (load - coup_of(1, r) * w.astype(jnp.float32)).astype(jnp.bfloat16)
        mid_start(f, mixed, dmid, dm_send, dm_recv)

    def down_second(f):
        mid_finish(f, mixed, dmid, dm_send, dm_recv)
        for r in range(rows):
            wb[f, r] = apply_row(1, r).astype(jnp.bfloat16)
        depth_start(f, din, wb, d_send, d_recv, 1)

    def emit(layer, f, r, value):
        s = value.astype(jnp.bfloat16)
        front = front_of(f)
        out_ref[layer, 0, front, pl.ds(r * blk, blk)] = s[:shots]
        out_ref[layer, 1, front, pl.ds(r * blk, blk)] = s[shots:]
        return (coup_of(layer, r) * s.astype(jnp.float32)).astype(jnp.bfloat16)

    def up_first(f):
        @pl.when(d < depth_count - 1)
        def _():
            depth_wait(f, uin, hout, u_send, u_recv, 1)
            for r in range(rows):
                ext[REACH + r] = uin[f, REACH + r]
            for side in (0, 1):
                @pl.when(valid(0, -to_dl(side)))
                def _():
                    for i in range(REACH):
                        e = i if side == 0 else REACH + rows + i
                        ext[e] = uin[f, e]
            for r in range(rows):
                handed[f, r] = emit(1, f, r, wb[f, r].astype(jnp.float32) - apply_row(1, r))

        @pl.when(d == depth_count - 1)
        def _():
            for r in range(rows):
                handed[f, r] = emit(1, f, r, wb[f, r].astype(jnp.float32))

        mid_start(f, handed, umid, um_send, um_recv)

    def up_second(f):
        mid_finish(f, handed, umid, um_send, um_recv)
        for r in range(rows):
            hout[f, r] = emit(0, f, r, wa[f, r].astype(jnp.float32) - apply_row(0, r))
        depth_start(f, uin, hout, u_send, u_recv, -1)

    for side in (0, 1):
        @pl.when(valid(0, -to_dl(side)))
        def _():
            for which in (0, 1):
                pre_copy(side, which).wait_recv()

    def pipeline(first, second):
        @pl.loop(0, fronts + 1)
        def _(t):
            @pl.when(t < fronts)
            def _():
                first(t)

            @pl.when(t > 0)
            def _():
                second(t - 1)

    pipeline(down_first, down_second)
    pipeline(up_first, up_second)

    for side in (0, 1):
        @pl.when(valid(0, to_dl(side)))
        def _():
            for which in (0, 1):
                pre_copy(side, which).wait_send()

    @pl.loop(0, fronts)
    def _(f):
        for side in (0, 1):
            @pl.when(valid(0, to_dl(side)))
            def _():
                mid_copy(f, side, mixed, dmid, dm_send, dm_recv).wait_send()
                mid_copy(f, side, handed, umid, um_send, um_recv).wait_send()
        for slot in (0, 1, 2):
            @pl.when(valid(1, 1 - slot))
            def _():
                depth_copy(f, slot, wb, din, d_send, d_recv, 1).wait_send()

            @pl.when(valid(-1, 1 - slot))
            def _():
                depth_copy(f, slot, hout, uin, u_send, u_recv, -1).wait_send()


def per_device(right_sides, sources, coupling, block_cols, factors):
    layers, parts, shot_count, cells = right_sides.shape
    rows, stored = block_cols.shape[1:]
    blk = factors.shape[-1]
    assert layers == 2 and rows >= REACH and parts == 2
    fronts = FRONTS
    pair = parts * (shot_count // fronts)
    ext_rows = rows + 2 * REACH
    bf16 = jnp.bfloat16
    spread = jnp.broadcast_to(sources[:, None], (shot_count, blk))
    vmem = pl.BlockSpec(memory_space=pltpu.VMEM)
    smem = pl.BlockSpec(memory_space=pltpu.SMEM)
    dma = pltpu.SemaphoreType.DMA
    return pl.pallas_call(
        functools.partial(sweep_kernel, lax.axis_size("depth"), lax.axis_size("lat"), fronts),
        out_shape=jax.ShapeDtypeStruct(right_sides.shape, bf16),
        in_specs=[smem, vmem, vmem, vmem, vmem],
        out_specs=vmem,
        scratch_shapes=[
            pltpu.VMEM((ext_rows, pair, blk), bf16),
            pltpu.VMEM((fronts, ext_rows, pair, blk), bf16),
            pltpu.VMEM((fronts, ext_rows, pair, blk), bf16),
            pltpu.VMEM((fronts, 2, REACH, pair, blk), bf16),
            pltpu.VMEM((fronts, 2, REACH, pair, blk), bf16),
            pltpu.VMEM((fronts, rows, pair, blk), bf16),
            pltpu.VMEM((fronts, rows, pair, blk), bf16),
            pltpu.VMEM((fronts, rows, pair, blk), bf16),
            pltpu.VMEM((fronts, rows, pair, blk), bf16),
            pltpu.VMEM((fronts, rows, pair, blk), bf16),
            pltpu.VMEM((2, parts, shot_count, REACH * blk), bf16),
            pltpu.VMEM((2, layers, REACH * blk), jnp.float32),
            dma((fronts, 3)), dma((fronts, 3)), dma((fronts, 3)), dma((fronts, 3)),
            dma((fronts, 2)), dma((fronts, 2)), dma((fronts, 2)), dma((fronts, 2)),
            dma((4,)), dma((4,)),
        ],
        compiler_params=pltpu.CompilerParams(collective_id=0, has_side_effects=True),
    )(block_cols.reshape(layers, rows * stored), spread, right_sides, coupling, factors)


def solution(mesh):
    in_specs = (
        P("depth", None, None, "lat"),
        P(),
        P("depth", "lat"),
        P("depth", "lat", None),
        P("depth", "lat", None, None, None, None),
    )
    out_specs = P("depth", None, None, "lat")
    return jax.shard_map(
        per_device, mesh=mesh, in_specs=in_specs, out_specs=out_specs, check_vma=False
    )
```

time: 617 us -> 134 us (0.22); the launches traced: 607 us -> 134 us
  starting transfers between devices: 335 us -> 0 us
  Pallas kernels: 0 us -> 130 us
  other arithmetic: 128 us -> 0 us
  waiting for transfers between devices: 72 us -> 0 us
  local copies, waits for them, and re-layouts: 60.2 us -> 4.54 us
    ppermute x110 -> x0, starting transfers between devices: 335 us -> none  [the longest x44 183 us: extended_2(): lax.ppermute(lax.slice_in_dim(block, block.shape[dim] - width, None, axis...]
    pallas_call x0 -> x1, Pallas kernels: none -> 130 us  [per_device(): pl.pallas_call(functools.partial(sweep_kernel, lax.axis_size('depth'), la...]
    ppermute x110 -> x0, waiting for transfers between devices: 72 us -> none  [the longest x22 61.8 us: from_behind(): return lax.ppermute(block, axis, route)]
    dynamic_update_slice x44 -> x0, other arithmetic: 64.1 us -> none  [place(): lax.dynamic_update_slice(stored, chosen, (layer_idx, 0, front_start, 0))]
    convert_element_type x59 -> x0, other arithmetic: 38 us -> none  [the longest x22 19.4 us: down_turn(): mixed_in = (source_load - coupling[layer_idx][None, None, :] * previous.a...]
    slice x88 -> x0, local copies, waits for them, and re-layouts: 32.2 us -> none  [the longest x11 19.9 us: up_turn(): stored[layer_idx]]
    and x16 -> x0, other arithmetic: 10.3 us -> none  [apply_factor(): jnp.take(pieces, offsets[layer_idx], axis=2)]
    gather x16 -> x0, local copies, waits for them, and re-layouts: 9.61 us -> none  [apply_factor(): jnp.take(pieces, offsets[layer_idx], axis=2)]
  transfers between devices with their start and end apart: 110 -> 0, of which waited for: 22 -> 0; matrix products, arithmetic and copies ran while one was open for 14% -> 0% of each run, Pallas kernels for 0% -> 0%
where the time goes in v1:
time: 134 us
  Pallas kernels  130 us (97%)
  local copies, waits for them, and re-layouts  4.54 us (3%)
    pallas_call x1, Pallas kernels, per_device(): pl.pallas_call(functools.partial(sweep_kernel, lax.axis_size('depth'), la...  130 us

profile of v1, /device:TPU:1, one launch (start us, length us, event | category | flops | bytes accessed | tf_op | source)
XLA Modules:
  0.0 134.2 jit_solution(4773930716292192323)
XLA Ops:
  0.0 0.8 copy.7
  0.8 0.7 reshape.4.cols_ref
  1.4 1.3 %broadcast_in_dim.2.srcs_ref = s32[64,128]{1,0:T(8,128)} broadcast(s32[64]{0:T(128)} %param.6), dimensions={0} | broadcast | bytes 33024 | tf_op jit(solution)/shard_map/broadcast_in_dim | solution.py:274
  2.8 129.6 %shard_map.55 = bf16[2,2,64,768]{3,2,1,0:T(8,128)(2,1)} custom-call(s32[2,24]{1,0:T(2,128)} %reshape.4.cols_ref, s32[64,128]{1,0:T(8,128)} %broadcast_in_dim.2.srcs_ref, bf16[2,2,64,768]{3,2,1,0:T(8,128)(2,1)} %rhs_ref.1, f32[2,768]{1,0:T(2,128)} %coup_ref.1, bf16[2,6,4,2,128,128]{5,4,3,2,1,0:T(8,128)(2,1)} %fac_ref.1), custom_call_target="tpu_custom_call" | custom-call | tf_op jit(solution)/shard_map/pallas_call | solution.py:278
  132.4 1.8 %copy.9 = bf16[2,2,64,768]{3,2,1,0:T(8,128)(2,1)} copy(bf16[2,2,64,768]{3,2,1,0:T(8,128)(2,1)} %shard_map.55) | data formatting | bytes 786432
